TPU v7x, 256 devices: a whole 4x4x8 slice. The times are simulated.
256 devices in a mesh: occi: 8 (over x_lo, y), occj: 32 (over z, x_hi, core).
Axes of the slice: x: 4 (x_hi: 2, x_lo: 2; x = x_hi * 2 + x_lo), y: 4, z: 8, core: 2. Of those that a mesh axis runs over, the one named last changes fastest.
Arguments:
- amplitudes: bfloat16 [64, 64, 256, 256], P('occi', 'occj'), may hold values from -6 to 6
- exchange: bfloat16 [64, 64, 256, 256], P('occi', 'occj'), may hold values from -6 to 6
- fock_virt: bfloat16 [256, 256], replicated, may hold values from -0.375 to 0.375
- intersection: bfloat16 [256, 256], replicated, may hold values from -0.1875 to 0.1875
- transform: bfloat16 [256, 256], replicated, may hold values from -0.375 to 0.375
- virt_energy: float32 [256], replicated, may hold values from 0.5 to 4
- occ_energy: float32 [64], replicated, may hold values from -1.5 to -0.3
- partners: int32 [64, 2], replicated, may hold values from 0 to 63, as said below
- coupling: float32 [64, 2], replicated, may hold values from -0.6 to 0.6
- domain: int32 [64, 8], replicated, may hold values 0 or 1
Outputs:
- residual: float32 [64, 64, 256, 256], P('occi', 'occj')
- new_amplitudes: bfloat16 [64, 64, 256, 256], P('occi', 'occj')
Inputs may be any that keep to these rules, and one draw needn't show every extreme that they name: The 2 partners of orbital i are distinct, differ from i, and lie within 2 of i; the first lies exactly 2 away.
All inputs are finite; a program needn't handle non-finite values.
Results may differ from a plain program's by a relative error of at most 0.0085.
Values may be sent and summed in bfloat16 or wider, within the bound.
No kernel may reach another device: no remote copies, remote signals or barrier semaphores. Data moves between devices by JAX's collectives and lax.ppermute only.
A program may use at most 128 MiB of HBM per device.

v0:
```python
import jax
import jax.numpy as jnp
from jax import lax
from jax.sharding import PartitionSpec as P

REACH = 2


def extended_2(block, sides, width):
    for axis, dim in sides:
        count = lax.axis_size(axis)
        forward = [(i, i + 1) for i in range(count - 1)]
        backward = [(target, source) for source, target in forward]
        low = lax.ppermute(
            lax.slice_in_dim(block, block.shape[dim] - width, None, axis=dim), axis, forward
        )
        high = lax.ppermute(lax.slice_in_dim(block, 0, width, axis=dim), axis, backward)
        block = jnp.concatenate([low, block, high], axis=dim)
    return block


def flip_blocks(block):
    rows_i = block.shape[0]
    cols_j = block.shape[1]
    width = block.shape[2]
    count_i = lax.axis_size("occi")
    count_j = lax.axis_size("occj")
    group = count_j // count_i
    slab = width // count_j
    moved = lax.all_to_all(
        block.reshape(1, rows_i, cols_j, width, width),
        "occj",
        split_axis=3,
        concat_axis=0,
        tiled=True,
    )
    moved = lax.all_to_all(
        moved.reshape(count_j, 1, rows_i, cols_j, slab, width),
        "occi",
        split_axis=0,
        concat_axis=1,
        tiled=True,
    )
    moved = moved.reshape(group, count_j, cols_j, cols_j, 1, slab, width)
    moved = lax.all_to_all(moved, "occj", split_axis=1, concat_axis=4, tiled=True)
    moved = moved.reshape(group, cols_j, cols_j, width, width)
    return jnp.transpose(moved, (0, 2, 1, 4, 3)).reshape(rows_i, cols_j, width, width)


def mix_rows(extended, lists, weights, start):
    local = lists - start + REACH
    total = jnp.zeros((lists.shape[0],) + extended.shape[1:], jnp.float32)
    for slot in range(lists.shape[1]):
        picked = jnp.take(extended, local[:, slot], axis=0).astype(jnp.float32)
        total = total + weights[:, slot, None, None, None] * picked
    return total


def mix_columns(extended, lists, weights, start):
    local = lists - start + REACH
    shape = (extended.shape[0], lists.shape[0]) + extended.shape[2:]
    total = jnp.zeros(shape, jnp.float32)
    for slot in range(lists.shape[1]):
        picked = jnp.take(extended, local[:, slot], axis=1).astype(jnp.float32)
        total = total + weights[None, :, slot, None, None] * picked
    return total


def per_device(
    amplitudes,
    exchange,
    fock_virt,
    intersection,
    transform,
    virt_energy,
    occ_energy,
    partners,
    coupling,
    domain,
):
    rows_i = amplitudes.shape[0]
    cols_j = amplitudes.shape[1]
    width = amplitudes.shape[2]
    tiles = domain.shape[1]
    start_i = lax.axis_index("occi") * rows_i
    start_j = lax.axis_index("occj") * cols_j
    intersection_full = (
        jnp.eye(width, dtype=jnp.float32) + intersection.astype(jnp.float32)
    ).astype(jnp.bfloat16)
    a1 = jnp.einsum(
        "ab,rsbc->rsac", fock_virt, amplitudes, preferred_element_type=jnp.float32
    ).astype(jnp.bfloat16)
    first = jnp.einsum("rsab,bc->rsac", a1, intersection_full, preferred_element_type=jnp.float32)
    a2 = jnp.einsum(
        "ab,rsbc->rsac", intersection_full, amplitudes, preferred_element_type=jnp.float32
    ).astype(jnp.bfloat16)
    second = jnp.einsum("rsab,bc->rsac", a2, fock_virt, preferred_element_type=jnp.float32)
    mirror = flip_blocks(amplitudes)
    sym = (0.5 * (amplitudes.astype(jnp.float32) + mirror.astype(jnp.float32))).astype(jnp.bfloat16)
    lists_i = lax.dynamic_slice_in_dim(partners, start_i, rows_i, 0)
    weights_i = lax.dynamic_slice_in_dim(coupling, start_i, rows_i, 0)
    extended_i = extended_2(sym, (("occi", 0),), REACH)
    c_row = mix_rows(extended_i, lists_i, weights_i, start_i).astype(jnp.bfloat16)
    lists_j = lax.dynamic_slice_in_dim(partners, start_j, cols_j, 0)
    weights_j = lax.dynamic_slice_in_dim(coupling, start_j, cols_j, 0)
    extended_j = extended_2(sym, (("occj", 1),), REACH)
    c_col = mix_columns(extended_j, lists_j, weights_j, start_j).astype(jnp.bfloat16)
    coup = c_row.astype(jnp.float32) + c_col.astype(jnp.float32)
    masks = jnp.repeat(domain.astype(jnp.float32), width // tiles, axis=1)
    mask_i = lax.dynamic_slice_in_dim(masks, start_i, rows_i, 0)
    mask_j = lax.dynamic_slice_in_dim(masks, start_j, cols_j, 0)
    mpair = jnp.maximum(mask_i[:, None, :], mask_j[None, :, :])
    two = mpair[:, :, :, None] * mpair[:, :, None, :]
    cmask = (coup * two).astype(jnp.bfloat16)
    b1 = jnp.einsum(
        "ab,rsbc->rsac", intersection_full, cmask, preferred_element_type=jnp.float32
    ).astype(jnp.bfloat16)
    third = jnp.einsum("rsab,bc->rsac", b1, intersection_full, preferred_element_type=jnp.float32)
    residual = two * (exchange.astype(jnp.float32) + first + second - third)
    resid_b = residual.astype(jnp.bfloat16)
    q1 = jnp.einsum("ba,rsbc->rsac", transform, resid_b, preferred_element_type=jnp.float32).astype(
        jnp.bfloat16
    )
    q2 = jnp.einsum("rsab,bc->rsac", q1, transform, preferred_element_type=jnp.float32)
    occ_i = lax.dynamic_slice_in_dim(occ_energy, start_i, rows_i, 0)
    occ_j = lax.dynamic_slice_in_dim(occ_energy, start_j, cols_j, 0)
    pair_shift = occ_i[:, None] + occ_j[None, :]
    denom = (
        virt_energy[None, None, :, None]
        + virt_energy[None, None, None, :]
        - pair_shift[:, :, None, None]
    )
    zeta = (q2 / denom).astype(jnp.bfloat16)
    u1 = jnp.einsum("ab,rsbc->rsac", transform, zeta, preferred_element_type=jnp.float32).astype(
        jnp.bfloat16
    )
    u2 = jnp.einsum("rsab,cb->rsac", u1, transform, preferred_element_type=jnp.float32)
    fresh = (amplitudes.astype(jnp.float32) - u2).astype(jnp.bfloat16)
    return (residual, fresh)


def solution(mesh):
    return jax.shard_map(
        per_device,
        mesh=mesh,
        in_specs=(
            P("occi", "occj", None, None),
            P("occi", "occj", None, None),
            P(),
            P(),
            P(),
            P(),
            P(),
            P(),
            P(),
            P(),
        ),
        out_specs=(P("occi", "occj", None, None), P("occi", "occj", None, None)),
        check_vma=False,
    )
```

profile of v0, /device:TPU:3, one launch (start us, length us, event | category | flops | bytes accessed | tf_op | source)
XLA Modules:
  0.0 281.1 jit_solution(13498421750724093916)
XLA Ops:
  0.6 3.8 %copy.94 = bf16[8,2,256,256]{3,1,0,2:T(2,128)(2,1)S(1)} copy(bf16[8,2,256,256]{3,2,1,0:T(8,128)(2,1)} %param.14) | data formatting | bytes 4194304 | tf_op args[0]
  4.4 61.2 %all_to_all.42 = bf16[1,8,2,256,256]{4,2,1,0,3:T(2,128)(2,1)S(1)} all-to-all(bf16[1,8,2,256,256]{4,2,1,0,3:T(2,128)(2,1)S(1)} %bitcast.98), channel_id=1, replica_groups=mesh['occi'=8,'occj'=32] {'occj'}, dimensions={3} | all-to-all | bytes 4194304 | tf_op jit(solution)/shard_map/all_to_all | solution.py:30
  66.6 29.6 %all_to_all.43 = bf16[32,1,8,2,8,256]{5,4,3,2,1,0:T(8,128)(2,1)S(1)} all-to-all(bf16[32,1,8,2,8,256]{5,4,3,2,1,0:T(8,128)(2,1)S(1)} %copy.56), channel_id=1, replica_groups=mesh['occi'=8,'occj'=32] {'occi'}, dimensions={0} | all-to-all | bytes 4194304 | tf_op jit(solution)/shard_map/all_to_all | solution.py:37
  98.0 7.9 %all-to-all-start.2 = ((bf16[4,32,2,2,1,8,256]{6,5,3,2,0,4,1:T(8,128)(2,1)}), bf16[4,32,2,2,1,8,256]{6,5,3,2,0,4,1:T(8,128)(2,1)S(1)}, u32[]{:S(2)}, u32[]{:S(2)}) async-start(bf16[4,32,2,2,1,8,256]{6,5,3,2,0,4,1:T(8,128)(2,1)} %copy.58), calls=%async_computation.2 | async-start | bytes 4194304 | tf_op jit(solution)/shard_map/all_to_all | solution.py:45
  106.9 49.1 %all-to-all-done.2 = bf16[4,32,2,2,1,8,256]{6,5,3,2,0,4,1:T(8,128)(2,1)S(1)} async-done(((bf16[4,32,2,2,1,8,256]{6,5,3,2,0,4,1:T(8,128)(2,1)}), bf16[4,32,2,2,1,8,256]{6,5,3,2,0,4,1:T(8,128)(2,1)S(1)}, u32[]{:S(2)}, u32[]{:S(2)}) %all-to-all-start.2) | async-done | bytes 2097184 | tf_op jit(solution)/shard_map/all_to_all | solution.py:45
  156.0 2.4 convert_bitcast_fusion
  158.4 5.4 %copy.60 = f32[4,2,2,256,256]{4,3,2,1,0:T(8,128)} copy(f32[4,2,2,256,256]{3,4,1,2,0:T(8,128)} %convert_bitcast_fusion) | data formatting | bytes 8388608 | tf_op jit(solution)/shard_map/convert_element_type | solution.py:99
  163.8 4.2 %fusion.1 = bf16[8,2,256,256]{3,2,1,0:T(8,128)(2,1)} fusion(bf16[8,2,256,256]{3,2,1,0:T(8,128)(2,1)S(1)} %copy-done.2, f32[4,2,2,256,256]{4,3,2,1,0:T(8,128)} %copy.60), kind=kLoop, calls=%fused_computation.10 | loop fusion | flops 4194304 | bytes 8388608 | tf_op jit(solution)/shard_map/convert_element_type | solution.py:99
  168.0 5.1 %collective-permute-start.2 = (bf16[8,2,256,256]{3,2,1,0:T(8,128)(2,1)}, bf16[8,2,256,256]{3,2,1,0:T(8,128)(2,1)}, u32[]{:S(2)}, u32[]{:S(2)}) collective-permute-start(bf16[8,2,256,256]{3,2,1,0:T(8,128)(2,1)} %fusion.1), channel_id=1, source_target_pairs={{0,1},{1,2},{2,3},{3,4},{4,5},{5,6},{6,7},{7,8},{8,9},{9,10},{10,1... | collective-permute-start | bytes 6291464 | tf_op jit(solution)/shard_map/ppermute | solution.py:14
  175.9 4.1 %fusion.10 = f32[8,2,256,256]{3,2,1,0:T(8,128)} fusion(bf16[8,2,256,256]{3,2,1,0:T(8,128)(2,1)S(1)} %copy-done.2, bf16[256,256]{1,0:T(8,128)(2,1)S(1)} %copy-done, bf16[256,256]{1,0:T(8,128)(2,1)S(1)} %copy-done.3), kind=kOutput, calls=%fused_computation.24 | convolution fusion | flops 1075118080 | bytes 6553600 | tf_op jit(solution)/shard_map/rsab,bc->rsac/dot_general | solution.py:93
  180.0 2.3 fusion.74
  182.2 2.2 collective-permute-start
  184.4 5.4 %collective-permute-start.1 = (bf16[2,2,256,256]{3,2,1,0:T(8,128)(2,1)}, bf16[2,2,256,256]{3,2,1,0:T(8,128)(2,1)S(1)}, u32[]{:S(2)}, u32[]{:S(2)}) collective-permute-start(bf16[2,2,256,256]{3,2,1,0:T(8,128)(2,1)} %get-tuple-element.13), channel_id=1, source_target_pairs={{32,0},{64,32},{96,64},{128,96},{160,128},{192,160},{224,192},{33,... | collective-permute-start | bytes 1572872 | tf_op jit(solution)/shard_map/ppermute | solution.py:17
  189.8 3.3 %fusion.8 = f32[8,2,256,256]{3,2,1,0:T(8,128)} fusion(bf16[8,2,256,256]{3,2,1,0:T(8,128)(2,1)S(1)} %copy-done.2, bf16[256,256]{1,0:T(8,128)(2,1)S(1)} %copy-done, bf16[256,256]{1,0:T(8,128)(2,1)S(1)} %copy-done.3), kind=kOutput, calls=%fused_computation.22 | convolution fusion | flops 1075118080 | bytes 6553600 | tf_op jit(solution)/shard_map/rsab,bc->rsac/dot_general | solution.py:97
  193.1 39.3 %collective-permute-done = bf16[2,2,256,256]{3,2,1,0:T(8,128)(2,1)S(1)} collective-permute-done((bf16[2,2,256,256]{3,2,1,0:T(8,128)(2,1)}, bf16[2,2,256,256]{3,2,1,0:T(8,128)(2,1)S(1)}, u32[]{:S(2)}, u32[]{:S(2)}) %collective-permute-start) | collective-permute-done | bytes 524320 | tf_op jit(solution)/shard_map/ppermute | solution.py:14
  232.4 3.0 %pad_maximum_fusion.1 = bf16[12,2,256,256]{3,2,1,0:T(8,128)(2,1)} fusion(bf16[2,2,256,256]{3,2,1,0:T(8,128)(2,1)S(1)} %collective-permute-done.1, bf16[8,2,256,256]{3,2,1,0:T(8,128)(2,1)} %fusion.1, bf16[2,2,256,256]{3,2,1,0:T(8,128)(2,1)S(1)} %collective-permute-done), kind=kLoop, calls=%fused_computation.17 | loop fusion | flops 3145728 | bytes 6291456 | tf_op jit(solution)/shard_map/concatenate | solution.py:18
  235.5 3.9 %gather_fusion = bf16[8,2,256,256]{3,2,1,0:T(8,128)(2,1)} fusion(bf16[12,2,256,256]{3,2,1,0:T(8,128)(2,1)} %pad_maximum_fusion.1, s32[1024]{0:T(1024)S(1)} %get-tuple-element.25), kind=kCustom, calls=%fused_computation.clone | custom fusion | bytes 4194336 | tf_op jit(solution)/shard_map/jit(_take)/gather | solution.py:54
  239.4 3.9 %gather_fusion.1 = bf16[8,2,256,256]{3,2,1,0:T(8,128)(2,1)} fusion(bf16[12,2,256,256]{3,2,1,0:T(8,128)(2,1)} %pad_maximum_fusion.1, s32[1024]{0:T(1024)S(1)} %get-tuple-element.24), kind=kCustom, calls=%fused_computation.2.clone | custom fusion | bytes 4194336 | tf_op jit(solution)/shard_map/jit(_take)/gather | solution.py:54
  243.3 6.4 %pad_maximum_fusion = bf16[8,6,256,256]{3,2,1,0:T(8,128)(2,1)} fusion(bf16[8,2,256,256]{3,2,1,0:T(8,128)(2,1)} %collective-permute-done.3, bf16[8,2,256,256]{3,2,1,0:T(8,128)(2,1)} %fusion.1, bf16[8,2,256,256]{3,2,1,0:T(8,128)(2,1)} %collective-permute-done.2), kind=kLoop, calls=%fused_computation.4 | loop fusion | flops 6291456 | bytes 12582912 | tf_op jit(solution)/shard_map/concatenate | solution.py:18
  249.7 4.8 %gather_fusion.2 = bf16[2,8,256,256]{3,2,1,0:T(8,128)(2,1)} fusion(bf16[8,6,256,256]{3,2,1,0:T(8,128)(2,1)} %pad_maximum_fusion, s32[1024]{0:T(1024)S(1)} %get-tuple-element.23), kind=kCustom, calls=%fused_computation.1.clone | custom fusion | bytes 4194312 | tf_op jit(solution)/shard_map/jit(_take)/gather | solution.py:64
  254.5 4.8 %gather_fusion.3 = bf16[2,8,256,256]{3,2,1,0:T(8,128)(2,1)} fusion(bf16[8,6,256,256]{3,2,1,0:T(8,128)(2,1)} %pad_maximum_fusion, s32[1024]{0:T(1024)S(1)} %get-tuple-element.22), kind=kCustom, calls=%fused_computation.3.clone | custom fusion | bytes 4194312 | tf_op jit(solution)/shard_map/jit(_take)/gather | solution.py:64
  259.3 10.0 %multiply_multiply_fusion = f32[8,2,256,256]{3,2,1,0:T(8,128)} fusion(f32[8,2,256,256]{3,2,1,0:T(8,128)} %fusion.8, f32[8,2,256,256]{3,2,1,0:T(8,128)} %fusion.10, bf16[8,2,256,256]{3,2,1,0:T(8,128)(2,1)} %param.15, bf16[2,8,256,256]{3,2,1,0:T(8,128)(2,1)} %gather_fusion.3, bf16[2,8,256,256]{3,2,1,0:T(8,128)(2,1)} %gather_fusion.2, ...), kind=kOutput, calls=%fused_computation.5 | convolution fusion | flops 1104805888 | bytes 23216228 | tf_op jit(solution)/shard_map/rsab,bc->rsac/dot_general | solution.py:118
  269.3 6.3 %fusion.5 = f32[8,2,256,256]{3,2,1,0:T(8,128)} fusion(f32[8,2,256,256]{3,2,1,0:T(8,128)} %multiply_multiply_fusion, bf16[256,256]{1,0:T(8,128)(2,1)S(1)} %copy-done.4), kind=kOutput, calls=%fused_computation.19 | convolution fusion | flops 1075838976 | bytes 8519680 | tf_op jit(solution)/shard_map/rsab,bc->rsac/dot_general | solution.py:124
  275.6 5.5 %fusion.2 = bf16[8,2,256,256]{3,2,1,0:T(8,128)(2,1)} fusion(bf16[8,2,256,256]{3,2,1,0:T(8,128)(2,1)S(1)} %copy-done.2, f32[8,2,256,256]{3,2,1,0:T(8,128)} %fusion.5, f32[8,2]{1,0:T(8,128)S(1)} %broadcast_add_fusion.1, f32[256,256]{1,0:T(8,128)S(1)} %copy-done.5, bf16[256,256]{1,0:T(8,128)(2,1)S(1)} %copy-done.4), kind=kOutput, calls=%fused_computation.11 | convolution fusion | flops 1081081856 | bytes 8781888 | tf_op jit(solution)/shard_map/rsab,cb->rsac/dot_general | solution.py:137
  (51 shorter events, 6.4 us)
Async XLA Ops:
  0.6 175.3 %copy-start = (bf16[256,256]{1,0:T(8,128)(2,1)S(1)}, bf16[256,256]{1,0:T(8,128)(2,1)}, u32[]{:S(2)}) copy-start(bf16[256,256]{1,0:T(8,128)(2,1)} %param.16) | copy-start | bytes 393220
  98.0 8.0 %copy-start.8 = (s32[64,8]{0,1:T(8,128)S(1)}, s32[64,8]{0,1:T(8,128)}, u32[]{:S(2)}) copy-start(s32[64,8]{0,1:T(8,128)} %param.23) | copy-start | bytes 6148
  98.0 8.2 %copy-start.10 = (f32[64]{0:T(128)S(1)}, f32[64]{0:T(128)}, u32[]{:S(2)}) copy-start(f32[64]{0:T(128)} %param.20) | copy-start | bytes 772
  98.0 8.5 %copy-start.7 = (s32[64,2]{0,1:T(2,128)S(1)}, s32[64,2]{0,1:T(2,128)}, u32[]{:S(2)}) copy-start(s32[64,2]{0,1:T(2,128)} %param.21) | copy-start | bytes 1540
  98.0 8.7 %copy-start.9 = (f32[64,2]{0,1:T(2,128)S(1)}, f32[64,2]{0,1:T(2,128)}, u32[]{:S(2)}) copy-start(f32[64,2]{0,1:T(2,128)} %param.22) | copy-start | bytes 1540
  98.0 58.0 %all-to-all-start.2 = ((bf16[4,32,2,2,1,8,256]{6,5,3,2,0,4,1:T(8,128)(2,1)}), bf16[4,32,2,2,1,8,256]{6,5,3,2,0,4,1:T(8,128)(2,1)S(1)}, u32[]{:S(2)}, u32[]{:S(2)}) async-start(bf16[4,32,2,2,1,8,256]{6,5,3,2,0,4,1:T(8,128)(2,1)} %copy.58), calls=%async_computation.2 | async-start | bytes 4194304 | tf_op jit(solution)/shard_map/all_to_all | solution.py:45
  158.4 5.4 %copy-start.2 = (bf16[8,2,256,256]{3,2,1,0:T(8,128)(2,1)S(1)}, bf16[8,2,256,256]{3,2,1,0:T(8,128)(2,1)}, u32[]{:S(2)}) copy-start(bf16[8,2,256,256]{3,2,1,0:T(8,128)(2,1)} %param.14) | copy-start | bytes 6291460
  163.8 11.3 %copy-start.6 = (f32[256]{0:T(256)S(1)}, f32[256]{0:T(256)}, u32[]{:S(2)}) copy-start(f32[256]{0:T(256)} %param.19) | copy-start | bytes 3076
  163.8 12.1 %copy-start.3 = (bf16[256,256]{1,0:T(8,128)(2,1)S(1)}, bf16[256,256]{1,0:T(8,128)(2,1)}, u32[]{:S(2)}) copy-start(bf16[256,256]{1,0:T(8,128)(2,1)} %param.17) | copy-start | bytes 393220
  168.0 75.3 %collective-permute-start.2 = (bf16[8,2,256,256]{3,2,1,0:T(8,128)(2,1)}, bf16[8,2,256,256]{3,2,1,0:T(8,128)(2,1)}, u32[]{:S(2)}, u32[]{:S(2)}) collective-permute-start(bf16[8,2,256,256]{3,2,1,0:T(8,128)(2,1)} %fusion.1), channel_id=1, source_target_pairs={{0,1},{1,2},{2,3},{3,4},{4,5},{5,6},{6,7},{7,8},{8,9},{9,10},{10,1... | collective-permute-start | bytes 6291464 | tf_op jit(solution)/shard_map/ppermute | solution.py:14
  173.1 70.2 %collective-permute-start.3 = (bf16[8,2,256,256]{3,2,1,0:T(8,128)(2,1)}, bf16[8,2,256,256]{3,2,1,0:T(8,128)(2,1)}, u32[]{:S(2)}, u32[]{:S(2)}) collective-permute-start(bf16[8,2,256,256]{3,2,1,0:T(8,128)(2,1)} %fusion.1), channel_id=1, source_target_pairs={{1,0},{2,1},{3,2},{4,3},{5,4},{6,5},{7,6},{8,7},{9,8},{10,9},{11,1... | collective-permute-start | bytes 6291464 | tf_op jit(solution)/shard_map/ppermute | solution.py:17
  182.2 50.2 %collective-permute-start = (bf16[2,2,256,256]{3,2,1,0:T(8,128)(2,1)}, bf16[2,2,256,256]{3,2,1,0:T(8,128)(2,1)S(1)}, u32[]{:S(2)}, u32[]{:S(2)}) collective-permute-start(bf16[2,2,256,256]{3,2,1,0:T(8,128)(2,1)} %get-tuple-element.12), channel_id=1, source_target_pairs={{0,32},{32,64},{64,96},{96,128},{128,160},{160,192},{192,224},{1,3... | collective-permute-start | bytes 1572872 | tf_op jit(solution)/shard_map/ppermute | solution.py:14
  184.4 48.0 %collective-permute-start.1 = (bf16[2,2,256,256]{3,2,1,0:T(8,128)(2,1)}, bf16[2,2,256,256]{3,2,1,0:T(8,128)(2,1)S(1)}, u32[]{:S(2)}, u32[]{:S(2)}) collective-permute-start(bf16[2,2,256,256]{3,2,1,0:T(8,128)(2,1)} %get-tuple-element.13), channel_id=1, source_target_pairs={{32,0},{64,32},{96,64},{128,96},{160,128},{192,160},{224,192},{33,... | collective-permute-start | bytes 1572872 | tf_op jit(solution)/shard_map/ppermute | solution.py:17
  259.3 10.0 %copy-start.4 = (bf16[256,256]{1,0:T(8,128)(2,1)S(1)}, bf16[256,256]{1,0:T(8,128)(2,1)}, u32[]{:S(2)}) copy-start(bf16[256,256]{1,0:T(8,128)(2,1)} %param.18) | copy-start | bytes 393220
  269.3 6.3 %copy-start.5 = (f32[256,256]{1,0:T(8,128)S(1)}, f32[256,256]{1,0:T(8,128)}, u32[]{:S(2)}) copy-start(f32[256,256]{1,0:T(8,128)} %broadcast_add_fusion) | copy-start | bytes 786436
  275.6 5.5 %copy-start.1 = (bf16[256,256]{1,0:T(8,128)(2,1)S(1)}, bf16[256,256]{1,0:T(8,128)(2,1)}, u32[]{:S(2)}) copy-start(bf16[256,256]{1,0:T(8,128)(2,1)} %param.16) | copy-start | bytes 393220
where the time goes:
time: 282 us; the launch traced here: 281 us
  blocking collectives  90.8 us (32%)
  waiting for transfers between devices  88.4 us (31%)
  local copies, waits for them, and re-layouts  32.2 us (11%)
  matrix products  29.2 us (10%)
  starting transfers between devices  22.5 us (8%)
  other arithmetic  17.1 us (6%)
    all_to_all x1, blocking collectives, flip_blocks(): lax.all_to_all(block.reshape(1, rows_i, cols_j, width, width), 'occj', sp...  61.2 us
    all_to_all x1, waiting for transfers between devices, flip_blocks(): lax.all_to_all(moved, 'occj', split_axis=1, concat_axis=4, tiled=True)  49.1 us
    ppermute x2, waiting for transfers between devices, extended_2(): lax.ppermute(lax.slice_in_dim(block, block.shape[dim] - width, None, axis...  39.3 us
    all_to_all x1, blocking collectives, flip_blocks(): lax.all_to_all(moved.reshape(count_j, 1, rows_i, cols_j, slab, width), 'o...  29.6 us
    dot_general x1, matrix products, per_device(): jnp.einsum('rsab,bc->rsac', b1, intersection_full, preferred_element_type...  10 us
    gather x2, local copies, waits for them, and re-layouts, mix_columns(): picked = jnp.take(extended, local[:, slot], axis=1).astype(jnp.float32)  9.58 us
    concatenate x2, other arithmetic, extended_2(): block = jnp.concatenate([low, block, high], axis=dim)  9.47 us
    all_to_all x1, starting transfers between devices, flip_blocks(): lax.all_to_all(moved, 'occj', split_axis=1, concat_axis=4, tiled=True)  7.93 us
  transfers between devices with their start and end apart: 5, of which 2 were waited for; matrix products, arithmetic and copies ran while one was open for 8% of the time, Pallas kernels for 0%

commit v1 on v0

--- a/solution.py
+++ b/solution.py
@@ -42,7 +42,10 @@
         tiled=True,
     )
     moved = moved.reshape(group, count_j, cols_j, cols_j, 1, slab, width)
-    moved = lax.all_to_all(moved, "occj", split_axis=1, concat_axis=4, tiled=True)
+    size = lax.axis_size("occj")
+    pieces = jnp.stack(jnp.split(moved, size, axis=1), axis=0)
+    pieces = lax.all_to_all(pieces, "occj", split_axis=0, concat_axis=0)
+    moved = jnp.concatenate(pieces, axis=4)
     moved = moved.reshape(group, cols_j, cols_j, width, width)
     return jnp.transpose(moved, (0, 2, 1, 4, 3)).reshape(rows_i, cols_j, width, width)
 

time: 282 us -> 301 us (1.067)
  local copies, waits for them, and re-layouts: 32.2 us -> 50.9 us
    unnamed x23 -> x54, local copies, waits for them, and re-layouts: 3.83 us -> 23.5 us
  transfers between devices with their start and end apart: 5 -> 5, of which waited for: 2 -> 2; matrix products, arithmetic and copies ran while one was open for 8% -> 7% of each run, Pallas kernels for 0% -> 0%
where the time goes in v1:
time: 301 us; the launch traced here: 300 us
  blocking collectives  90.8 us (30%)
  waiting for transfers between devices  88.4 us (29%)
  local copies, waits for them, and re-layouts  50.9 us (17%)
  matrix products  29.2 us (10%)
  starting transfers between devices  22.5 us (7%)
  other arithmetic  17.1 us (6%)
    all_to_all x1, blocking collectives, flip_blocks(): lax.all_to_all(block.reshape(1, rows_i, cols_j, width, width), 'occj', sp...  61.2 us
    all_to_all x1, waiting for transfers between devices, flip_blocks(): pieces = lax.all_to_all(pieces, 'occj', split_axis=0, concat_axis=0)  49.1 us
    ppermute x2, waiting for transfers between devices, extended_2(): lax.ppermute(lax.slice_in_dim(block, block.shape[dim] - width, None, axis...  39.3 us
    all_to_all x1, blocking collectives, flip_blocks(): lax.all_to_all(moved.reshape(count_j, 1, rows_i, cols_j, slab, width), 'o...  29.6 us
    unnamed x54, local copies, waits for them, and re-layouts  23.5 us
    dot_general x1, matrix products, per_device(): jnp.einsum('rsab,bc->rsac', b1, intersection_full, preferred_element_type...  10 us
    gather x2, local copies, waits for them, and re-layouts, mix_columns(): picked = jnp.take(extended, local[:, slot], axis=1).astype(jnp.float32)  9.58 us
    concatenate x2, other arithmetic, extended_2(): block = jnp.concatenate([low, block, high], axis=dim)  9.47 us
  transfers between devices with their start and end apart: 5, of which 2 were waited for; matrix products, arithmetic and copies ran while one was open for 7% of the time, Pallas kernels for 0%

profile of v1, /device:TPU:3, one launch (start us, length us, event | category | flops | bytes accessed | tf_op | source)
XLA Modules:
  0.0 299.9 jit_solution(7278975571713075359)
XLA Ops:
  0.6 3.8 %copy.274 = bf16[8,2,256,256]{3,1,0,2:T(2,128)(2,1)S(1)} copy(bf16[8,2,256,256]{3,2,1,0:T(8,128)(2,1)} %param.14) | data formatting | bytes 4194304 | tf_op args[0]
  4.4 61.2 %all_to_all.35 = bf16[1,8,2,256,256]{4,2,1,0,3:T(2,128)(2,1)S(1)} all-to-all(bf16[1,8,2,256,256]{4,2,1,0,3:T(2,128)(2,1)S(1)} %bitcast.315), channel_id=1, replica_groups=mesh['occi'=8,'occj'=32] {'occj'}, dimensions={3} | all-to-all | bytes 4194304 | tf_op jit(solution)/shard_map/all_to_all | solution.py:30
  66.6 29.6 %all_to_all.36 = bf16[32,1,8,2,8,256]{5,4,3,2,1,0:T(8,128)(2,1)S(1)} all-to-all(bf16[32,1,8,2,8,256]{5,4,3,2,1,0:T(8,128)(2,1)S(1)} %copy.177), channel_id=1, replica_groups=mesh['occi'=8,'occj'=32] {'occi'}, dimensions={0} | all-to-all | bytes 4194304 | tf_op jit(solution)/shard_map/all_to_all | solution.py:37
  116.8 7.9 %all-to-all-start.2 = ((bf16[32,4,1,2,2,1,8,256]{7,6,4,3,1,5,2,0:T(8,128)(2,1)}), bf16[32,4,1,2,2,1,8,256]{7,6,4,3,1,5,2,0:T(8,128)(2,1)S(1)}, u32[]{:S(2)}, u32[]{:S(2)}) async-start(bf16[32,4,1,2,2,1,8,256]{7,6,4,3,1,5,2,0:T(8,128)(2,1)} %fusion.68), calls=%async_computation.2 | async-start | bytes 4194304 | tf_op jit(solution)/shard_map/all_to_all | solution.py:47
  125.7 49.1 %all-to-all-done.2 = bf16[32,4,1,2,2,1,8,256]{7,6,4,3,1,5,2,0:T(8,128)(2,1)S(1)} async-done(((bf16[32,4,1,2,2,1,8,256]{7,6,4,3,1,5,2,0:T(8,128)(2,1)}), bf16[32,4,1,2,2,1,8,256]{7,6,4,3,1,5,2,0:T(8,128)(2,1)S(1)}, u32[]{:S(2)}, u32[]{:S(2)}) %all-to-all-start.2) | async-done | bytes 2097184 | tf_op jit(solution)/shard_map/all_to_all | solution.py:47
  174.8 2.4 copy_bitcast_fusion
  177.2 5.4 %copy.210 = f32[4,2,2,256,256]{4,3,2,1,0:T(8,128)} copy(f32[4,2,2,256,256]{3,4,1,2,0:T(8,128)} %copy_bitcast_fusion) | data formatting | bytes 8388608 | tf_op jit(solution)/shard_map/convert_element_type | solution.py:102
  182.6 4.2 %fusion.1 = bf16[8,2,256,256]{3,2,1,0:T(8,128)(2,1)} fusion(bf16[8,2,256,256]{3,2,1,0:T(8,128)(2,1)S(1)} %copy-done.2, f32[4,2,2,256,256]{4,3,2,1,0:T(8,128)} %copy.210), kind=kLoop, calls=%fused_computation.10 | loop fusion | flops 4194304 | bytes 8388608 | tf_op jit(solution)/shard_map/convert_element_type | solution.py:102
  186.7 5.1 %collective-permute-start.2 = (bf16[8,2,256,256]{3,2,1,0:T(8,128)(2,1)}, bf16[8,2,256,256]{3,2,1,0:T(8,128)(2,1)}, u32[]{:S(2)}, u32[]{:S(2)}) collective-permute-start(bf16[8,2,256,256]{3,2,1,0:T(8,128)(2,1)} %fusion.1), channel_id=1, source_target_pairs={{0,1},{1,2},{2,3},{3,4},{4,5},{5,6},{6,7},{7,8},{8,9},{9,10},{10,1... | collective-permute-start | bytes 6291464 | tf_op jit(solution)/shard_map/ppermute | solution.py:14
  194.7 4.1 %fusion.10 = f32[8,2,256,256]{3,2,1,0:T(8,128)} fusion(bf16[8,2,256,256]{3,2,1,0:T(8,128)(2,1)S(1)} %copy-done.2, bf16[256,256]{1,0:T(8,128)(2,1)S(1)} %copy-done, bf16[256,256]{1,0:T(8,128)(2,1)S(1)} %copy-done.3), kind=kOutput, calls=%fused_computation.25 | convolution fusion | flops 1075118080 | bytes 6553600 | tf_op jit(solution)/shard_map/rsab,bc->rsac/dot_general | solution.py:96
  198.7 2.3 fusion.106
  201.0 2.2 collective-permute-start
  203.2 5.4 %collective-permute-start.1 = (bf16[2,2,256,256]{3,2,1,0:T(8,128)(2,1)}, bf16[2,2,256,256]{3,2,1,0:T(8,128)(2,1)S(1)}, u32[]{:S(2)}, u32[]{:S(2)}) collective-permute-start(bf16[2,2,256,256]{3,2,1,0:T(8,128)(2,1)} %get-tuple-element.13), channel_id=1, source_target_pairs={{32,0},{64,32},{96,64},{128,96},{160,128},{192,160},{224,192},{33,... | collective-permute-start | bytes 1572872 | tf_op jit(solution)/shard_map/ppermute | solution.py:17
  208.6 3.3 %fusion.8 = f32[8,2,256,256]{3,2,1,0:T(8,128)} fusion(bf16[8,2,256,256]{3,2,1,0:T(8,128)(2,1)S(1)} %copy-done.2, bf16[256,256]{1,0:T(8,128)(2,1)S(1)} %copy-done, bf16[256,256]{1,0:T(8,128)(2,1)S(1)} %copy-done.3), kind=kOutput, calls=%fused_computation.23 | convolution fusion | flops 1075118080 | bytes 6553600 | tf_op jit(solution)/shard_map/rsab,bc->rsac/dot_general | solution.py:100
  211.9 39.3 %collective-permute-done = bf16[2,2,256,256]{3,2,1,0:T(8,128)(2,1)S(1)} collective-permute-done((bf16[2,2,256,256]{3,2,1,0:T(8,128)(2,1)}, bf16[2,2,256,256]{3,2,1,0:T(8,128)(2,1)S(1)}, u32[]{:S(2)}, u32[]{:S(2)}) %collective-permute-start) | collective-permute-done | bytes 524320 | tf_op jit(solution)/shard_map/ppermute | solution.py:14
  251.2 3.0 %pad_maximum_fusion.1 = bf16[12,2,256,256]{3,2,1,0:T(8,128)(2,1)} fusion(bf16[2,2,256,256]{3,2,1,0:T(8,128)(2,1)S(1)} %collective-permute-done.1, bf16[8,2,256,256]{3,2,1,0:T(8,128)(2,1)} %fusion.1, bf16[2,2,256,256]{3,2,1,0:T(8,128)(2,1)S(1)} %collective-permute-done), kind=kLoop, calls=%fused_computation.18 | loop fusion | flops 3145728 | bytes 6291456 | tf_op jit(solution)/shard_map/concatenate | solution.py:18
  254.2 3.9 %gather_fusion = bf16[8,2,256,256]{3,2,1,0:T(8,128)(2,1)} fusion(bf16[12,2,256,256]{3,2,1,0:T(8,128)(2,1)} %pad_maximum_fusion.1, s32[1024]{0:T(1024)S(1)} %get-tuple-element.25), kind=kCustom, calls=%fused_computation.clone | custom fusion | bytes 4194336 | tf_op jit(solution)/shard_map/jit(_take)/gather | solution.py:57
  258.1 3.9 %gather_fusion.1 = bf16[8,2,256,256]{3,2,1,0:T(8,128)(2,1)} fusion(bf16[12,2,256,256]{3,2,1,0:T(8,128)(2,1)} %pad_maximum_fusion.1, s32[1024]{0:T(1024)S(1)} %get-tuple-element.24), kind=kCustom, calls=%fused_computation.2.clone | custom fusion | bytes 4194336 | tf_op jit(solution)/shard_map/jit(_take)/gather | solution.py:57
  262.0 6.4 %pad_maximum_fusion = bf16[8,6,256,256]{3,2,1,0:T(8,128)(2,1)} fusion(bf16[8,2,256,256]{3,2,1,0:T(8,128)(2,1)} %collective-permute-done.3, bf16[8,2,256,256]{3,2,1,0:T(8,128)(2,1)} %fusion.1, bf16[8,2,256,256]{3,2,1,0:T(8,128)(2,1)} %collective-permute-done.2), kind=kLoop, calls=%fused_computation.4 | loop fusion | flops 6291456 | bytes 12582912 | tf_op jit(solution)/shard_map/concatenate | solution.py:18
  268.5 4.8 %gather_fusion.2 = bf16[2,8,256,256]{3,2,1,0:T(8,128)(2,1)} fusion(bf16[8,6,256,256]{3,2,1,0:T(8,128)(2,1)} %pad_maximum_fusion, s32[1024]{0:T(1024)S(1)} %get-tuple-element.23), kind=kCustom, calls=%fused_computation.1.clone | custom fusion | bytes 4194312 | tf_op jit(solution)/shard_map/jit(_take)/gather | solution.py:67
  273.3 4.8 %gather_fusion.3 = bf16[2,8,256,256]{3,2,1,0:T(8,128)(2,1)} fusion(bf16[8,6,256,256]{3,2,1,0:T(8,128)(2,1)} %pad_maximum_fusion, s32[1024]{0:T(1024)S(1)} %get-tuple-element.22), kind=kCustom, calls=%fused_computation.3.clone | custom fusion | bytes 4194312 | tf_op jit(solution)/shard_map/jit(_take)/gather | solution.py:67
  278.0 10.0 %multiply_multiply_fusion = f32[8,2,256,256]{3,2,1,0:T(8,128)} fusion(f32[8,2,256,256]{3,2,1,0:T(8,128)} %fusion.8, f32[8,2,256,256]{3,2,1,0:T(8,128)} %fusion.10, bf16[8,2,256,256]{3,2,1,0:T(8,128)(2,1)} %param.15, bf16[2,8,256,256]{3,2,1,0:T(8,128)(2,1)} %gather_fusion.3, bf16[2,8,256,256]{3,2,1,0:T(8,128)(2,1)} %gather_fusion.2, ...), kind=kOutput, calls=%fused_computation.5 | convolution fusion | flops 1104805888 | bytes 23216228 | tf_op jit(solution)/shard_map/rsab,bc->rsac/dot_general | solution.py:121
  288.1 6.3 %fusion.5 = f32[8,2,256,256]{3,2,1,0:T(8,128)} fusion(f32[8,2,256,256]{3,2,1,0:T(8,128)} %multiply_multiply_fusion, bf16[256,256]{1,0:T(8,128)(2,1)S(1)} %copy-done.4), kind=kOutput, calls=%fused_computation.20 | convolution fusion | flops 1075838976 | bytes 8519680 | tf_op jit(solution)/shard_map/rsab,bc->rsac/dot_general | solution.py:127
  294.4 5.5 %fusion.2 = bf16[8,2,256,256]{3,2,1,0:T(8,128)(2,1)} fusion(bf16[8,2,256,256]{3,2,1,0:T(8,128)(2,1)S(1)} %copy-done.2, f32[8,2,256,256]{3,2,1,0:T(8,128)} %fusion.5, f32[8,2]{1,0:T(8,128)S(1)} %broadcast_add_fusion.1, f32[256,256]{1,0:T(8,128)S(1)} %copy-done.5, bf16[256,256]{1,0:T(8,128)(2,1)S(1)} %copy-done.4), kind=kOutput, calls=%fused_computation.11 | convolution fusion | flops 1081081856 | bytes 8781888 | tf_op jit(solution)/shard_map/rsab,cb->rsac/dot_general | solution.py:140
  (82 shorter events, 25.2 us)
Async XLA Ops:
  0.6 194.0 %copy-start = (bf16[256,256]{1,0:T(8,128)(2,1)S(1)}, bf16[256,256]{1,0:T(8,128)(2,1)}, u32[]{:S(2)}) copy-start(bf16[256,256]{1,0:T(8,128)(2,1)} %param.16) | copy-start | bytes 393220
  116.8 8.0 %copy-start.8 = (s32[64,8]{0,1:T(8,128)S(1)}, s32[64,8]{0,1:T(8,128)}, u32[]{:S(2)}) copy-start(s32[64,8]{0,1:T(8,128)} %param.23) | copy-start | bytes 6148
  116.8 8.2 %copy-start.10 = (f32[64]{0:T(128)S(1)}, f32[64]{0:T(128)}, u32[]{:S(2)}) copy-start(f32[64]{0:T(128)} %param.20) | copy-start | bytes 772
  116.8 8.5 %copy-start.7 = (s32[64,2]{0,1:T(2,128)S(1)}, s32[64,2]{0,1:T(2,128)}, u32[]{:S(2)}) copy-start(s32[64,2]{0,1:T(2,128)} %param.21) | copy-start | bytes 1540
  116.8 8.7 %copy-start.9 = (f32[64,2]{0,1:T(2,128)S(1)}, f32[64,2]{0,1:T(2,128)}, u32[]{:S(2)}) copy-start(f32[64,2]{0,1:T(2,128)} %param.22) | copy-start | bytes 1540
  116.8 58.0 %all-to-all-start.2 = ((bf16[32,4,1,2,2,1,8,256]{7,6,4,3,1,5,2,0:T(8,128)(2,1)}), bf16[32,4,1,2,2,1,8,256]{7,6,4,3,1,5,2,0:T(8,128)(2,1)S(1)}, u32[]{:S(2)}, u32[]{:S(2)}) async-start(bf16[32,4,1,2,2,1,8,256]{7,6,4,3,1,5,2,0:T(8,128)(2,1)} %fusion.68), calls=%async_computation.2 | async-start | bytes 4194304 | tf_op jit(solution)/shard_map/all_to_all | solution.py:47
  177.2 5.4 %copy-start.2 = (bf16[8,2,256,256]{3,2,1,0:T(8,128)(2,1)S(1)}, bf16[8,2,256,256]{3,2,1,0:T(8,128)(2,1)}, u32[]{:S(2)}) copy-start(bf16[8,2,256,256]{3,2,1,0:T(8,128)(2,1)} %param.14) | copy-start | bytes 6291460
  182.6 11.3 %copy-start.6 = (f32[256]{0:T(256)S(1)}, f32[256]{0:T(256)}, u32[]{:S(2)}) copy-start(f32[256]{0:T(256)} %param.19) | copy-start | bytes 3076
  182.6 12.1 %copy-start.3 = (bf16[256,256]{1,0:T(8,128)(2,1)S(1)}, bf16[256,256]{1,0:T(8,128)(2,1)}, u32[]{:S(2)}) copy-start(bf16[256,256]{1,0:T(8,128)(2,1)} %param.17) | copy-start | bytes 393220
  186.7 75.3 %collective-permute-start.2 = (bf16[8,2,256,256]{3,2,1,0:T(8,128)(2,1)}, bf16[8,2,256,256]{3,2,1,0:T(8,128)(2,1)}, u32[]{:S(2)}, u32[]{:S(2)}) collective-permute-start(bf16[8,2,256,256]{3,2,1,0:T(8,128)(2,1)} %fusion.1), channel_id=1, source_target_pairs={{0,1},{1,2},{2,3},{3,4},{4,5},{5,6},{6,7},{7,8},{8,9},{9,10},{10,1... | collective-permute-start | bytes 6291464 | tf_op jit(solution)/shard_map/ppermute | solution.py:14
  191.9 70.2 %collective-permute-start.3 = (bf16[8,2,256,256]{3,2,1,0:T(8,128)(2,1)}, bf16[8,2,256,256]{3,2,1,0:T(8,128)(2,1)}, u32[]{:S(2)}, u32[]{:S(2)}) collective-permute-start(bf16[8,2,256,256]{3,2,1,0:T(8,128)(2,1)} %fusion.1), channel_id=1, source_target_pairs={{1,0},{2,1},{3,2},{4,3},{5,4},{6,5},{7,6},{8,7},{9,8},{10,9},{11,1... | collective-permute-start | bytes 6291464 | tf_op jit(solution)/shard_map/ppermute | solution.py:17
  201.0 50.2 %collective-permute-start = (bf16[2,2,256,256]{3,2,1,0:T(8,128)(2,1)}, bf16[2,2,256,256]{3,2,1,0:T(8,128)(2,1)S(1)}, u32[]{:S(2)}, u32[]{:S(2)}) collective-permute-start(bf16[2,2,256,256]{3,2,1,0:T(8,128)(2,1)} %get-tuple-element.12), channel_id=1, source_target_pairs={{0,32},{32,64},{64,96},{96,128},{128,160},{160,192},{192,224},{1,3... | collective-permute-start | bytes 1572872 | tf_op jit(solution)/shard_map/ppermute | solution.py:14
  203.2 48.0 %collective-permute-start.1 = (bf16[2,2,256,256]{3,2,1,0:T(8,128)(2,1)}, bf16[2,2,256,256]{3,2,1,0:T(8,128)(2,1)S(1)}, u32[]{:S(2)}, u32[]{:S(2)}) collective-permute-start(bf16[2,2,256,256]{3,2,1,0:T(8,128)(2,1)} %get-tuple-element.13), channel_id=1, source_target_pairs={{32,0},{64,32},{96,64},{128,96},{160,128},{192,160},{224,192},{33,... | collective-permute-start | bytes 1572872 | tf_op jit(solution)/shard_map/ppermute | solution.py:17
  278.0 10.0 %copy-start.4 = (bf16[256,256]{1,0:T(8,128)(2,1)S(1)}, bf16[256,256]{1,0:T(8,128)(2,1)}, u32[]{:S(2)}) copy-start(bf16[256,256]{1,0:T(8,128)(2,1)} %param.18) | copy-start | bytes 393220
  288.1 6.3 %copy-start.5 = (f32[256,256]{1,0:T(8,128)S(1)}, f32[256,256]{1,0:T(8,128)}, u32[]{:S(2)}) copy-start(f32[256,256]{1,0:T(8,128)} %broadcast_add_fusion) | copy-start | bytes 786436
  294.4 5.5 %copy-start.1 = (bf16[256,256]{1,0:T(8,128)(2,1)S(1)}, bf16[256,256]{1,0:T(8,128)(2,1)}, u32[]{:S(2)}) copy-start(bf16[256,256]{1,0:T(8,128)(2,1)} %param.16) | copy-start | bytes 393220
